TPU v7x, 32 devices: a whole 2x2x4 slice. The times are simulated.
32 devices in a mesh: dp: 16 (over z, y, x), expert: 2 (over core).
Axes of the slice: x: 2, y: 2, z: 4, core: 2. Of those that a mesh axis runs over, the one named last changes fastest.
Arguments:
- latents: bfloat16 [4096, 2048], P('dp', 'expert'), as said below
- cotangent: bfloat16 [4096, 2048], P('dp', 'expert'), may hold values from -6 to 6
- routes: int32 [4096, 2], P('dp'), may hold values from 0 to 15, all different within a row; in each aligned block of 256 rows (0 to 255, 256 to 511, ...) at most 48 rows name the same one
- router_w: float32 [2048, 16], P('expert'), may hold values from -1 to 1
- mod_shift: bfloat16 [1, 2048], P(None, 'expert'), may hold values from -3 to 3
- mod_scale: bfloat16 [1, 2048], P(None, 'expert'), may hold values from -1.5 to 2.5
- mod_gate: bfloat16 [1, 2048], P(None, 'expert'), may hold values from -4 to 4
- gate_w: bfloat16 [16, 2048, 1024], P('dp', None, 'expert'), may hold values from -0.125 to 0.125
- up_w: bfloat16 [16, 2048, 1024], P('dp', None, 'expert'), may hold values from -0.125 to 0.125
- down_w: bfloat16 [16, 1024, 2048], P('dp', 'expert'), may hold values from -0.1875 to 0.1875
Outputs:
- latent_gradient: bfloat16 [4096, 2048], P('dp', 'expert')
- grad_gate_w: bfloat16 [16, 2048, 1024], P('dp', None, 'expert')
- grad_up_w: bfloat16 [16, 2048, 1024], P('dp', None, 'expert')
- grad_down_w: bfloat16 [16, 1024, 2048], P('dp', 'expert')
- grad_router: float32 [2048, 16], P('expert')
Inputs may be any that keep to these rules, and one draw needn't show every extreme that they name: `routes`: the two experts of a token differ. Among the 256 tokens of one aligned block (the tokens of one index of dp), no expert is named more than 48 times, a bound that some block reaches. Columns and rows of latents have unlike scales.
All inputs are finite; a program needn't handle non-finite values.
Results may differ from a plain program's by a relative error of at most 0.008.
Values may be sent and summed in bfloat16 or wider, within the bound.
No kernel may reach another device: no remote copies, remote signals or barrier semaphores. Data moves between devices by JAX's collectives and lax.ppermute only.
A program may use at most 128 MiB of HBM per device.

v0:
```python
import jax
import jax.numpy as jnp
from jax import lax
from jax.sharding import PartitionSpec as P

SEQ = 4096
norm_eps = 1e-06


def slot_targets(routes, experts, capacity):
    flat_routes = routes.reshape(-1)
    expert_ids = jnp.arange(experts, dtype=jnp.int32)
    onehot = (flat_routes[:, None] == expert_ids[None, :]).astype(jnp.int32)
    rank_run = jnp.cumsum(onehot, axis=0) - 1
    return flat_routes * capacity + jnp.sum(onehot * rank_run, axis=1)


def selected_row(table, sample_index):
    return lax.dynamic_slice_in_dim(table, sample_index, 1, 0).astype(jnp.float32)


def owner_view(arrived, groups, local):
    shaped = arrived.reshape((groups, local) + arrived.shape[1:])
    shaped = jnp.swapaxes(shaped, 0, 1)
    return shaped.reshape((local, groups * arrived.shape[1]) + arrived.shape[2:])


def sender_view(outgoing, groups):
    local = outgoing.shape[0]
    capacity = outgoing.shape[1] // groups
    shaped = outgoing.reshape((local, groups, capacity) + outgoing.shape[2:])
    shaped = jnp.swapaxes(shaped, 0, 1)
    return shaped.reshape((groups * local, capacity) + outgoing.shape[2:])


def route_weights(logits, routes, experts):
    chances = jax.nn.sigmoid(logits)
    expert_ids = jnp.arange(experts, dtype=jnp.int32)
    hits = routes[:, :, None] == expert_ids[None, None, :]
    picked = jnp.sum(jnp.where(hits, chances[:, None, :], 0.0), axis=2)
    pick_sum = jnp.sum(picked, axis=1, keepdims=True)
    return (hits, picked, pick_sum, picked / pick_sum)


def fill_slots(rows_b, scaled_dy, weights_b, targets, slot_count):
    width_here = rows_b.shape[1]
    send_x = (
        jnp.zeros((slot_count, width_here), jnp.bfloat16)
        .at[targets]
        .set(jnp.repeat(rows_b, 2, axis=0))
    )
    send_z = (
        jnp.zeros((slot_count, width_here), jnp.bfloat16)
        .at[targets]
        .set(jnp.repeat(scaled_dy, 2, axis=0))
    )
    send_w = jnp.zeros((slot_count,), jnp.bfloat16).at[targets].set(weights_b.reshape(-1))
    return (send_x, send_z, send_w)


def expert_grads(gate_lin, up_lin, down_back, slot_w):
    gate_sig = jax.nn.sigmoid(gate_lin)
    gate_act = gate_lin * gate_sig
    hidden = gate_act * up_lin
    slot_score = jnp.sum(hidden * down_back, axis=-1)
    d_gate = down_back * up_lin * gate_sig * (1.0 + gate_lin * (1.0 - gate_sig))
    d_up = down_back * gate_act
    scale_col = slot_w.astype(jnp.float32)[..., None]
    return (
        d_gate.astype(jnp.bfloat16),
        d_up.astype(jnp.bfloat16),
        slot_score,
        (scale_col * d_gate).astype(jnp.bfloat16),
        (scale_col * d_up).astype(jnp.bfloat16),
        (scale_col * hidden).astype(jnp.bfloat16),
    )


def weight_grads(rows_x, rows_z, gate_wt, up_wt, hidden_wt):
    grad_gate = jnp.einsum(
        "esd,esh->edh", rows_x, gate_wt, preferred_element_type=jnp.float32
    ).astype(jnp.bfloat16)
    grad_up = jnp.einsum("esd,esh->edh", rows_x, up_wt, preferred_element_type=jnp.float32).astype(
        jnp.bfloat16
    )
    grad_down = jnp.einsum(
        "esh,esd->ehd", hidden_wt, rows_z, preferred_element_type=jnp.float32
    ).astype(jnp.bfloat16)
    return (grad_gate, grad_up, grad_down)


def slot_total(slot_score):
    return lax.psum(slot_score, "expert")


def finish_tokens(
    returned_rows,
    score_rows,
    hits,
    picked,
    pick_sum,
    weights,
    normed_part,
    centered_scaled_slice,
    amp_part,
    inverse_deviation,
    output_gradient_slice,
    router_w,
    entire_width,
):
    highest = lax.Precision.HIGHEST
    tok_rows = weights.shape[0]
    paired = returned_rows.reshape(tok_rows, 2, -1)
    combined = weights[:, 0:1] * paired[:, 0] + weights[:, 1:2] * paired[:, 1]
    score_pair = score_rows.reshape(tok_rows, 2)
    mean_score = jnp.sum(weights * score_pair, axis=1, keepdims=True)
    d_pick = (score_pair - mean_score) / pick_sum * picked * (1.0 - picked)
    dlogit = jnp.sum(jnp.where(hits, d_pick[:, :, None], 0.0), axis=1)
    dnormed = combined + jnp.einsum("te,de->td", dlogit, router_w, precision=highest)
    grad_router = lax.psum(jnp.einsum("td,te->de", normed_part, dlogit, precision=highest), "dp")
    normalized_gradient = dnormed * amp_part
    first_sum, second_sum = lax.psum(
        (
            jnp.sum(normalized_gradient, axis=1, keepdims=True),
            jnp.sum(normalized_gradient * centered_scaled_slice, axis=1, keepdims=True),
        ),
        "expert",
    )
    latent_gradient = (
        inverse_deviation
        * (
            normalized_gradient
            - first_sum / entire_width
            - centered_scaled_slice * (second_sum / entire_width)
        )
        + output_gradient_slice
    )
    return (latent_gradient.astype(jnp.bfloat16), grad_router)


def per_device(
    latents, cotangent, routes, router_w, mod_shift, mod_scale, mod_gate, gate_w, up_w, down_w
):
    highest = lax.Precision.HIGHEST
    tok_rows = latents.shape[0]
    slice_width = latents.shape[1]
    experts = router_w.shape[1]
    local = gate_w.shape[0]
    groups = lax.axis_size("dp")
    entire_width = slice_width * lax.axis_size("expert")
    capacity = 3 * tok_rows // experts
    slot_count = experts * capacity
    sample_index = lax.axis_index("dp") * tok_rows // SEQ
    column_offset = lax.axis_index("expert") * slice_width
    targets = slot_targets(routes, experts, capacity)
    output_gradient_slice = cotangent.astype(jnp.float32)
    whole_x, whole_dy, entire_shift, whole_scale, whole_gate = (
        lax.all_gather(latents, "expert", axis=1, tiled=True),
        lax.all_gather(cotangent, "expert", axis=1, tiled=True),
        lax.all_gather(mod_shift, "expert", axis=1, tiled=True),
        lax.all_gather(mod_scale, "expert", axis=1, tiled=True),
        lax.all_gather(mod_gate, "expert", axis=1, tiled=True),
    )
    router_full = lax.all_gather(
        router_w.astype(jnp.bfloat16), "expert", axis=0, tiled=True
    ).astype(router_w.dtype)
    latent_rows_f32 = whole_x.astype(jnp.float32)
    row_average = jnp.mean(latent_rows_f32, axis=1, keepdims=True)
    row_msq = jnp.mean(latent_rows_f32 * latent_rows_f32, axis=1, keepdims=True)
    inverse_deviation = lax.rsqrt(row_msq - row_average * row_average + norm_eps)
    centered_scaled = (latent_rows_f32 - row_average) * inverse_deviation
    modulation_amplitude = 1.0 + selected_row(whole_scale, sample_index)
    normed_rows = centered_scaled * modulation_amplitude + selected_row(entire_shift, sample_index)
    normed_b = normed_rows.astype(jnp.bfloat16)
    logits = jnp.dot(normed_rows, router_full, precision=highest)
    hits, picked, pick_sum, weights = route_weights(logits, routes, experts)
    scaled_dy = (selected_row(whole_gate, sample_index) * whole_dy.astype(jnp.float32)).astype(
        jnp.bfloat16
    )
    send_x, send_z, send_w = fill_slots(
        normed_b, scaled_dy, weights.astype(jnp.bfloat16), targets, slot_count
    )
    got_x, got_z, got_w = (
        lax.all_to_all(
            send_x.reshape(experts, capacity, entire_width),
            "dp",
            split_axis=0,
            concat_axis=0,
            tiled=True,
        ),
        lax.all_to_all(
            send_z.reshape(experts, capacity, entire_width),
            "dp",
            split_axis=0,
            concat_axis=0,
            tiled=True,
        ),
        lax.all_to_all(
            send_w.reshape(experts, capacity), "dp", split_axis=0, concat_axis=0, tiled=True
        ),
    )
    rows_x = owner_view(got_x, groups, local)
    rows_z = owner_view(got_z, groups, local)
    slot_w = owner_view(got_w, groups, local)
    gate_lin = jnp.einsum("esd,edh->esh", rows_x, gate_w, preferred_element_type=jnp.float32)
    up_lin = jnp.einsum("esd,edh->esh", rows_x, up_w, preferred_element_type=jnp.float32)
    down_back = jnp.einsum("esd,ehd->esh", rows_z, down_w, preferred_element_type=jnp.float32)
    d_gate_b, d_up_b, slot_score, gate_wt, up_wt, hidden_wt = expert_grads(
        gate_lin, up_lin, down_back, slot_w
    )
    grad_gate, grad_up, grad_down = weight_grads(rows_x, rows_z, gate_wt, up_wt, hidden_wt)
    part_rows = (
        jnp.einsum("esh,edh->esd", d_gate_b, gate_w, preferred_element_type=jnp.float32)
        + jnp.einsum("esh,edh->esd", d_up_b, up_w, preferred_element_type=jnp.float32)
    ).astype(jnp.bfloat16)
    score_sum = slot_total(slot_score)
    back_rows = lax.all_to_all(
        sender_view(part_rows, groups), "dp", split_axis=0, concat_axis=0, tiled=True
    )
    back_scores = lax.all_to_all(
        sender_view(score_sum, groups), "dp", split_axis=0, concat_axis=0, tiled=True
    )
    summed = lax.psum_scatter(
        back_rows.reshape(slot_count, entire_width).astype(jnp.float32).astype(jnp.bfloat16),
        "expert",
        scatter_dimension=1,
        tiled=True,
    ).astype(jnp.float32)
    returned_rows = summed[targets]
    score_rows = back_scores.reshape(-1)[targets]
    centered_scaled_slice = lax.dynamic_slice_in_dim(centered_scaled, column_offset, slice_width, 1)
    amp_part = lax.dynamic_slice_in_dim(modulation_amplitude, column_offset, slice_width, 1)
    normed_part = lax.dynamic_slice_in_dim(normed_rows, column_offset, slice_width, 1)
    latent_gradient, grad_router = finish_tokens(
        returned_rows,
        score_rows,
        hits,
        picked,
        pick_sum,
        weights,
        normed_part,
        centered_scaled_slice,
        amp_part,
        inverse_deviation,
        output_gradient_slice,
        router_w,
        entire_width,
    )
    return (latent_gradient, grad_gate, grad_up, grad_down, grad_router)


def solution(mesh):
    placed = (
        P("dp", "expert"),
        P("dp", "expert"),
        P("dp", None),
        P("expert", None),
        P(None, "expert"),
        P(None, "expert"),
        P(None, "expert"),
        P("dp", None, "expert"),
        P("dp", None, "expert"),
        P("dp", "expert", None),
    )
    return jax.shard_map(
        per_device,
        mesh=mesh,
        in_specs=placed,
        out_specs=(
            P("dp", "expert"),
            P("dp", None, "expert"),
            P("dp", None, "expert"),
            P("dp", "expert", None),
            P("expert", None),
        ),
        check_vma=False,
    )
```

profile of v0, /device:TPU:0, one launch (start us, length us, event | category | flops | bytes accessed | tf_op | source)
XLA Modules:
  0.0 442.6 jit_solution(14642404818928266631)
XLA Ops:
  15.6 5.7 %all-gather.3.cloned.1.call-done = bf16[256,2048]{1,0:T(8,128)(2,1)} async-done(((bf16[256,1024]{1,0:T(8,128)(2,1)}), bf16[256,2048]{1,0:T(8,128)(2,1)}) %all-gather.3.cloned.1.call-update) | async-done | bytes 1048592 | tf_op jit(solution)/shard_map/all_gather | solution.py:158
  23.0 3.8 multiply_add_fusion
  29.4 4.1 reshape.288
  33.5 6.7 %scatter_custom_fusion.1 = bf16[768,2048]{1,0:T(8,128)(2,1)} fusion(s32[512]{0:T(512)S(1)} %bitcast.91, bf16[512,2048]{1,0:T(8,128)(2,1)} %reshape.288, bf16[]{:T(256)} %constant.21.clone.1), kind=kCustom, calls=%fused_computation.35 | custom fusion | bytes 3146240 | tf_op jit(solution)/shard_map/scatter | solution.py:50
  40.3 7.0 %all-to-all-start.1 = ((bf16[16,48,2048]{2,1,0:T(8,128)(2,1)}), bf16[16,48,2048]{2,1,0:T(8,128)(2,1)}, u32[]{:S(2)}, u32[]{:S(2)}) async-start(bf16[16,48,2048]{2,1,0:T(8,128)(2,1)} %bitcast.82), calls=%async_computation.1 | async-start | bytes 6291456 | tf_op jit(solution)/shard_map/all_to_all | solution.py:184
  50.2 9.8 %all-gather.5.cloned.1.call-done = bf16[256,2048]{1,0:T(8,128)(2,1)} async-done(((bf16[256,1024]{1,0:T(8,128)(2,1)}), bf16[256,2048]{1,0:T(8,128)(2,1)}) %all-gather.5.cloned.1.call-update) | async-done | bytes 1048592 | tf_op jit(solution)/shard_map/all_gather | solution.py:159
  64.0 4.1 reshape.280
  68.1 6.7 %scatter_custom_fusion = bf16[768,2048]{1,0:T(8,128)(2,1)} fusion(s32[512]{0:T(512)S(1)} %bitcast.92, bf16[512,2048]{1,0:T(8,128)(2,1)} %reshape.280, bf16[]{:T(256)} %constant.21.clone.1), kind=kCustom, calls=%fused_computation.37 | custom fusion | bytes 3146240 | tf_op jit(solution)/shard_map/scatter | solution.py:55
  74.9 33.7 %all-to-all-done.1 = bf16[16,48,2048]{2,1,0:T(8,128)(2,1)} async-done(((bf16[16,48,2048]{2,1,0:T(8,128)(2,1)}), bf16[16,48,2048]{2,1,0:T(8,128)(2,1)}, u32[]{:S(2)}, u32[]{:S(2)}) %all-to-all-start.1) | async-done | bytes 3145760 | tf_op jit(solution)/shard_map/all_to_all | solution.py:184
  108.6 16.2 %all-to-all-start = ((bf16[16,48,2048]{2,1,0:T(8,128)(2,1)}), bf16[16,48,2048]{2,1,0:T(8,128)(2,1)}, u32[]{:S(2)}, u32[]{:S(2)}) async-start(bf16[16,48,2048]{2,1,0:T(8,128)(2,1)} %bitcast.83), calls=%async_computation | async-start | bytes 6291456 | tf_op jit(solution)/shard_map/all_to_all | solution.py:191
  125.4 5.0 %fusion.7 = f32[768,512]{0,1:T(8,128)} fusion(bf16[768,2048]{1,0:T(8,128)(2,1)} %bitcast.11, bf16[1,2048,512]{2,1,0:T(8,128)(2,1)S(1)} %copy-done), kind=kOutput, calls=%fused_computation.19 | convolution fusion | flops 1610612736 | bytes 6815744 | tf_op jit(solution)/shard_map/esd,edh->esh/dot_general | solution.py:205
  130.4 4.9 %fusion.10 = f32[768,512]{0,1:T(8,128)} fusion(bf16[768,2048]{1,0:T(8,128)(2,1)} %bitcast.11, bf16[1,2048,512]{2,1,0:T(8,128)(2,1)S(1)} %copy-done.8), kind=kOutput, calls=%fused_computation.22 | convolution fusion | flops 1610612736 | bytes 6815744 | tf_op jit(solution)/shard_map/esd,edh->esh/dot_general | solution.py:206
  135.3 50.2 %all-to-all-done = bf16[16,48,2048]{2,1,0:T(8,128)(2,1)} async-done(((bf16[16,48,2048]{2,1,0:T(8,128)(2,1)}), bf16[16,48,2048]{2,1,0:T(8,128)(2,1)}, u32[]{:S(2)}, u32[]{:S(2)}) %all-to-all-start) | async-done | bytes 3145760 | tf_op jit(solution)/shard_map/all_to_all | solution.py:191
  185.5 5.5 %multiply_reduce_fusion = (f32[768]{0:T(1024)S(1)}, f32[768,512]{0,1:T(8,128)S(1)}) fusion(f32[768,512]{0,1:T(8,128)} %fusion.10, f32[768,512]{0,1:T(8,128)} %fusion.7, bf16[768,2048]{1,0:T(8,128)(2,1)} %bitcast.8, bf16[1,512,2048]{2,1,0:T(8,128)(2,1)} %param.19), kind=kOutput, calls=%fused_computation.31 | convolution fusion | flops 1613364480 | bytes 9964544 | tf_op jit(solution)/shard_map/esd,ehd->esh/dot_general | solution.py:207
  195.4 84.8 %all_to_all.34 = bf16[16,48,2048]{2,1,0:T(8,128)(2,1)} all-to-all(bf16[16,48,2048]{2,1,0:T(8,128)(2,1)S(1)} %bitcast.84), channel_id=1, replica_groups=mesh['dp'=16,'expert'=2] {'dp'}, dimensions={0} | all-to-all | bytes 6291456 | tf_op jit(solution)/shard_map/all_to_all | solution.py:217
  284.9 3.8 scatter_custom_fusion.2
  289.3 4.0 all-to-all-start.4
  293.3 7.2 %all-to-all-done.4 = bf16[16,1,48]{2,1,0:T(2,128)(2,1)S(1)} async-done(((bf16[16,1,48]{2,1,0:T(2,128)(2,1)}), bf16[16,1,48]{2,1,0:T(2,128)(2,1)S(1)}, u32[]{:S(2)}, u32[]{:S(2)}) %all-to-all-start.4) | async-done | bytes 1568 | tf_op jit(solution)/shard_map/all_to_all | solution.py:198
  300.8 3.1 psum.28
  303.8 3.5 all-to-all-start.3
  307.6 6.2 %fusion.1 = bf16[1,2048,512]{2,1,0:T(8,128)(2,1)} fusion(bf16[768,2048]{1,0:T(8,128)(2,1)} %bitcast.11, f32[768]{0:T(1024)S(1)} %reshape.259, f32[768,512]{0,1:T(8,128)} %copy-done.12, f32[768,512]{0,1:T(8,128)} %fusion.7), kind=kOutput, calls=%fused_computation.13 | convolution fusion | flops 1614413824 | bytes 8391680 | tf_op jit(solution)/shard_map/esd,esh->edh/dot_general | solution.py:83
  313.9 5.2 %fusion = bf16[1,2048,512]{2,1,0:T(8,128)(2,1)} fusion(bf16[768,2048]{1,0:T(8,128)(2,1)} %bitcast.11, f32[768]{0:T(1024)S(1)} %reshape.259, f32[768,512]{0,1:T(8,128)S(1)} %copy-done.11, f32[768,512]{0,1:T(8,128)S(1)} %copy-done.13, f32[768,512]{0,1:T(8,128)S(1)} %copy-done.15), kind=kOutput, calls=%fused_computation.12 | convolution fusion | flops 1615986688 | bytes 9964544 | tf_op jit(solution)/shard_map/esd,esh->edh/dot_general | solution.py:80
  319.1 5.1 %fusion.2 = bf16[1,512,2048]{2,1,0:T(8,128)(2,1)} fusion(bf16[768,2048]{1,0:T(8,128)(2,1)} %bitcast.8, f32[768]{0:T(1024)S(1)} %reshape.259, f32[768,512]{0,1:T(8,128)S(1)} %copy-done.15, f32[768,512]{0,1:T(8,128)S(1)} %copy-done.11), kind=kOutput, calls=%fused_computation.14 | convolution fusion | flops 1614413824 | bytes 8391680 | tf_op jit(solution)/shard_map/esh,esd->ehd/dot_general | solution.py:86
  344.7 89.7 %all-reduce.3.cloned.1.call-done = f32[1024,16]{0,1:T(8,128)} async-done(((f32[1024,16]{0,1:T(8,128)}), f32[1024,16]{0,1:T(8,128)}) %all-reduce.3.cloned.1.call-update) | async-done | bytes 65552 | tf_op jit(solution)/shard_map/psum | solution.py:120
  (101 shorter events, 52.1 us)
Async XLA Ops:
  7.2 118.2 %copy-start = (bf16[1,2048,512]{2,1,0:T(8,128)(2,1)S(1)}, bf16[1,2048,512]{2,1,0:T(8,128)(2,1)}, u32[]{:S(2)}) copy-start(bf16[1,2048,512]{2,1,0:T(8,128)(2,1)} %param.17) | copy-start | bytes 6291460
  7.2 14.1 %all-gather.3.cloned.1.call-start = ((), (), s32[]{:S(2)}) async-start(), calls=%async_computation.6 | async-start | bytes 1572864 | tf_op jit(solution)/shard_map/all_gather | solution.py:158
  40.3 7.7 %copy-start.7 = (bf16[1,1024]{1,0:T(2,128)(2,1)S(1)}, bf16[1,1024]{1,0:T(2,128)(2,1)}, u32[]{:S(2)}) copy-start(bf16[1,1024]{1,0:T(2,128)(2,1)} %param.16) | copy-start | bytes 6148
  40.3 68.3 %all-to-all-start.1 = ((bf16[16,48,2048]{2,1,0:T(8,128)(2,1)}), bf16[16,48,2048]{2,1,0:T(8,128)(2,1)}, u32[]{:S(2)}, u32[]{:S(2)}) async-start(bf16[16,48,2048]{2,1,0:T(8,128)(2,1)} %bitcast.82), calls=%async_computation.1 | async-start | bytes 6291456 | tf_op jit(solution)/shard_map/all_to_all | solution.py:184
  47.3 12.7 %all-gather.5.cloned.1.call-start = ((), (), s32[]{:S(2)}) async-start(), calls=%async_computation.7 | async-start | bytes 1572864 | tf_op jit(solution)/shard_map/all_gather | solution.py:159
  108.6 76.9 %all-to-all-start = ((bf16[16,48,2048]{2,1,0:T(8,128)(2,1)}), bf16[16,48,2048]{2,1,0:T(8,128)(2,1)}, u32[]{:S(2)}, u32[]{:S(2)}) async-start(bf16[16,48,2048]{2,1,0:T(8,128)(2,1)} %bitcast.83), calls=%async_computation | async-start | bytes 6291456 | tf_op jit(solution)/shard_map/all_to_all | solution.py:191
  124.8 204.7 %reduce-scatter.2.cloned.1.call-start = ((), (), s32[]{:S(2)}) async-start(), calls=%async_computation.8 | async-start | bytes 4718592 | tf_op jit(solution)/shard_map/reduce_scatter | solution.py:223
  125.4 5.0 %copy-start.8 = (bf16[1,2048,512]{2,1,0:T(8,128)(2,1)S(1)}, bf16[1,2048,512]{2,1,0:T(8,128)(2,1)}, u32[]{:S(2)}) copy-start(bf16[1,2048,512]{2,1,0:T(8,128)(2,1)} %param.18) | copy-start | bytes 6291460
  185.5 5.5 %copy-start.10 = (f32[768,512]{0,1:T(8,128)S(1)}, f32[768,512]{0,1:T(8,128)}, u32[]{:S(2)}) copy-start(f32[768,512]{0,1:T(8,128)} %fusion.7) | copy-start | bytes 4718596
  185.5 5.6 %copy-start.14 = (f32[768,512]{0,1:T(8,128)S(1)}, f32[768,512]{0,1:T(8,128)}, u32[]{:S(2)}) copy-start(f32[768,512]{0,1:T(8,128)} %fusion.10) | copy-start | bytes 4718596
  191.1 2.4 copy-start.12
  191.1 2.3 copy-start.9
  280.2 0.8 copy-start.5
  280.2 2.9 copy-start.4
  280.2 4.3 copy-start.6
  289.3 11.2 %all-to-all-start.4 = ((bf16[16,1,48]{2,1,0:T(2,128)(2,1)}), bf16[16,1,48]{2,1,0:T(2,128)(2,1)S(1)}, u32[]{:S(2)}, u32[]{:S(2)}) async-start(bf16[16,1,48]{2,1,0:T(2,128)(2,1)} %all_to_all.28), calls=%async_computation.5 | async-start | bytes 16384 | tf_op jit(solution)/shard_map/all_to_all | solution.py:198
  303.8 20.3 %all-to-all-start.3 = ((f32[16,1,48]{2,1,0:T(1,128)}), f32[16,1,48]{2,1,0:T(1,128)S(1)}, u32[]{:S(2)}, u32[]{:S(2)}) async-start(f32[16,1,48]{2,1,0:T(1,128)} %psum.28), calls=%async_computation.4 | async-start | bytes 16384 | tf_op jit(solution)/shard_map/all_to_all | solution.py:220
  307.3 6.5 %copy-start.11 = (f32[768,512]{0,1:T(8,128)S(1)}, f32[768,512]{0,1:T(8,128)}, u32[]{:S(2)}) copy-start(f32[768,512]{0,1:T(8,128)} %fusion.7) | copy-start | bytes 4718596
  307.3 127.0 %all-reduce.3.cloned.1.call-start = ((), (), s32[]{:S(2)}) async-start(), calls=%async_computation.9 | async-start | bytes 131072 | tf_op jit(solution)/shard_map/psum | solution.py:120
  307.6 6.3 %copy-start.13 = (f32[768,512]{0,1:T(8,128)S(1)}, f32[768,512]{0,1:T(8,128)}, u32[]{:S(2)}) copy-start(f32[768,512]{0,1:T(8,128)} %copy-done.12) | copy-start | bytes 4718596
  307.6 6.3 %copy-start.15 = (f32[768,512]{0,1:T(8,128)S(1)}, f32[768,512]{0,1:T(8,128)}, u32[]{:S(2)}) copy-start(f32[768,512]{0,1:T(8,128)} %fusion.10) | copy-start | bytes 4718596
  324.2 4.0 copy-start.3
  336.5 1.6 copy-start.2
  338.2 97.7 %copy-start.1 = (bf16[1,2048,512]{2,1,0:T(8,128)(2,1)S(1)}, bf16[1,2048,512]{2,1,0:T(8,128)(2,1)}, u32[]{:S(2)}) copy-start(bf16[1,2048,512]{2,1,0:T(8,128)(2,1)} %param.17) | copy-start | bytes 6291460
Sparse Core Ops, SparseCore 0:
  9.5 11.7 all-gather.2
  49.6 10.2 all-gather.4
  280.3 9.3 reduce-scatter.1
  329.6 104.7 all-reduce.2
where the time goes:
time: 450 us; the launch traced here: 443 us
  waiting for transfers between devices  198 us (44%)
  blocking collectives  98.5 us (22%)
  local copies, waits for them, and re-layouts  45.6 us (10%)
  matrix products  40.5 us (9%)
  starting transfers between devices  31.5 us (7%)
  between operations  14.4 us (3%)
  other arithmetic  14.2 us (3%)
    psum x1, waiting for transfers between devices, finish_tokens(): lax.psum(jnp.einsum('td,te->de', normed_part, dlogit, precision=highest),...  89.7 us
    all_to_all x1, blocking collectives, per_device(): lax.all_to_all(sender_view(part_rows, groups), 'dp', split_axis=0, concat...  84.8 us
    all_to_all x1, waiting for transfers between devices, per_device(): lax.all_to_all(send_z.reshape(experts, capacity, entire_width), 'dp', spl...  50.2 us
    all_to_all x1, waiting for transfers between devices, per_device(): lax.all_to_all(send_x.reshape(experts, capacity, entire_width), 'dp', spl...  33.7 us
    all_to_all x1, starting transfers between devices, per_device(): lax.all_to_all(send_z.reshape(experts, capacity, entire_width), 'dp', spl...  16.2 us
    all_gather x1, waiting for transfers between devices, per_device(): lax.all_gather(cotangent, 'expert', axis=1, tiled=True)  9.78 us
  transfers between devices with their start and end apart: 8, of which 6 were waited for; matrix products, arithmetic and copies ran while one was open for 15% of the time, Pallas kernels for 0%

commit v1 on v0

--- a/solution.py
+++ b/solution.py
@@ -117,7 +117,10 @@
     d_pick = (score_pair - mean_score) / pick_sum * picked * (1.0 - picked)
     dlogit = jnp.sum(jnp.where(hits, d_pick[:, :, None], 0.0), axis=1)
     dnormed = combined + jnp.einsum("te,de->td", dlogit, router_w, precision=highest)
-    grad_router = lax.psum(jnp.einsum("td,te->de", normed_part, dlogit, precision=highest), "dp")
+    grad_router = jnp.sum(
+        lax.all_gather(jnp.einsum("td,te->de", normed_part, dlogit, precision=highest), "dp"),
+        axis=0,
+    )
     normalized_gradient = dnormed * amp_part
     first_sum, second_sum = lax.psum(
         (

time: 450 us -> 368 us (0.82)
  blocking collectives: 98.5 us -> 13.7 us
  waiting for transfers between devices: 198 us -> 161 us
  starting transfers between devices: 31.5 us -> 60.5 us
  matrix products: 40.5 us -> 49.1 us
    psum x1 -> x0, waiting for transfers between devices: 89.7 us -> none  [finish_tokens(): lax.psum(jnp.einsum('td,te->de', normed_part, dlogit, precision=highest),...]
    all_to_all x1 -> x0, blocking collectives: 84.8 us -> none  [per_device(): lax.all_to_all(sender_view(part_rows, groups), 'dp', split_axis=0, concat...]
    all_to_all x0 -> x1, waiting for transfers between devices: none -> 52.8 us  [per_device(): lax.all_to_all(sender_view(part_rows, groups), 'dp', split_axis=0, concat...]
    all_to_all x1, starting transfers between devices: 4.01 us -> 16 us  [per_device(): lax.all_to_all(send_w.reshape(experts, capacity), 'dp', split_axis=0, con...]
    all_to_all x1, starting transfers between devices: 3.47 us -> 14.1 us  [per_device(): lax.all_to_all(sender_view(score_sum, groups), 'dp', split_axis=0, concat...]
    all_to_all x0 -> x1, starting transfers between devices: none -> 7.03 us  [per_device(): lax.all_to_all(sender_view(part_rows, groups), 'dp', split_axis=0, concat...]
  transfers between devices with their start and end apart: 8 -> 9, of which waited for: 6 -> 6; matrix products, arithmetic and copies ran while one was open for 15% -> 19% of each run, Pallas kernels for 0% -> 0%
where the time goes in v1:
time: 368 us; the launch traced here: 361 us
  waiting for transfers between devices  161 us (44%)
  starting transfers between devices  60.5 us (16%)
  matrix products  49.1 us (13%)
  local copies, waits for them, and re-layouts  46.9 us (13%)
  other arithmetic  14.8 us (4%)
  between operations  14.4 us (4%)
  blocking collectives  13.7 us (4%)
    all_to_all x1, waiting for transfers between devices, per_device(): lax.all_to_all(sender_view(part_rows, groups), 'dp', split_axis=0, concat...  52.8 us
    all_to_all x1, waiting for transfers between devices, per_device(): lax.all_to_all(send_z.reshape(experts, capacity, entire_width), 'dp', spl...  50.8 us
    all_to_all x1, waiting for transfers between devices, per_device(): lax.all_to_all(send_x.reshape(experts, capacity, entire_width), 'dp', spl...  33.7 us
    all_to_all x1, starting transfers between devices, per_device(): lax.all_to_all(send_z.reshape(experts, capacity, entire_width), 'dp', spl...  16.2 us
    all_to_all x1, starting transfers between devices, per_device(): lax.all_to_all(send_w.reshape(experts, capacity), 'dp', split_axis=0, con...  16 us
    all_to_all x1, starting transfers between devices, per_device(): lax.all_to_all(sender_view(score_sum, groups), 'dp', split_axis=0, concat...  14.1 us
    all_gather x1, waiting for transfers between devices, per_device(): lax.all_gather(cotangent, 'expert', axis=1, tiled=True)  9.61 us
  transfers between devices with their start and end apart: 9, of which 6 were waited for; matrix products, arithmetic and copies ran while one was open for 19% of the time, Pallas kernels for 0%

profile of v1, /device:TPU:0, one launch (start us, length us, event | category | flops | bytes accessed | tf_op | source)
XLA Modules:
  0.0 360.8 jit_solution(1580853472096654611)
XLA Ops:
  15.6 5.7 %all-gather.5.cloned.1.call-done = bf16[256,2048]{1,0:T(8,128)(2,1)} async-done(((bf16[256,1024]{1,0:T(8,128)(2,1)}), bf16[256,2048]{1,0:T(8,128)(2,1)}) %all-gather.5.cloned.1.call-update) | async-done | bytes 1048592 | tf_op jit(solution)/shard_map/all_gather | solution.py:161
  23.0 3.8 %multiply_add_fusion = (f32[256,2048]{1,0:T(8,128)}, bf16[256,2048]{1,0:T(8,128)(2,1)S(1)}, f32[256,2048]{1,0:T(8,128)}) fusion(f32[2048]{0:T(1024)S(1)} %bitcast.93, f32[2048]{0:T(1024)S(1)} %bitcast.91, f32[256]{0:T(256)S(1)} %get-tuple-element.23, f32[256]{0:T(256)S(1)} %get-tuple-element.22, bf16[256,2048]{1,0:T(8,128)(2,1)} %all-gather.5.cloned.1.call-done), kind=kLoop, calls=%fused_computation.27 | loop fusion | flops 3145728 | bytes 6309888 | tf_op jit(solution)/shard_map/add | solution.py:176
  29.4 4.1 %reshape.288 = bf16[512,2048]{1,0:T(8,128)(2,1)} reshape(bf16[256,2,2048]{2,1,0:T(2,128)(2,1)} %broadcast_in_dim.35) | data formatting | bytes 4194304 | tf_op jit(solution)/shard_map/reshape | solution.py:50
  33.5 6.7 %scatter_custom_fusion.1 = bf16[768,2048]{1,0:T(8,128)(2,1)} fusion(s32[512]{0:T(512)S(1)} %bitcast.97, bf16[512,2048]{1,0:T(8,128)(2,1)} %reshape.288, bf16[]{:T(256)} %constant.21.clone.1), kind=kCustom, calls=%fused_computation.35 | custom fusion | bytes 3146240 | tf_op jit(solution)/shard_map/scatter | solution.py:50
  40.2 7.0 %all-to-all-start.1 = ((bf16[16,48,2048]{2,1,0:T(8,128)(2,1)}), bf16[16,48,2048]{2,1,0:T(8,128)(2,1)}, u32[]{:S(2)}, u32[]{:S(2)}) async-start(bf16[16,48,2048]{2,1,0:T(8,128)(2,1)} %bitcast.87), calls=%async_computation.1 | async-start | bytes 6291456 | tf_op jit(solution)/shard_map/all_to_all | solution.py:187
  50.3 9.6 %all-gather.7.cloned.1.call-done = bf16[256,2048]{1,0:T(8,128)(2,1)} async-done(((bf16[256,1024]{1,0:T(8,128)(2,1)}), bf16[256,2048]{1,0:T(8,128)(2,1)}) %all-gather.7.cloned.1.call-update) | async-done | bytes 1048592 | tf_op jit(solution)/shard_map/all_gather | solution.py:162
  64.0 4.1 %reshape.280 = bf16[512,2048]{1,0:T(8,128)(2,1)} reshape(bf16[256,2,2048]{2,1,0:T(2,128)(2,1)} %broadcast_in_dim.34) | data formatting | bytes 4194304 | tf_op jit(solution)/shard_map/reshape | solution.py:55
  68.1 6.7 %scatter_custom_fusion = bf16[768,2048]{1,0:T(8,128)(2,1)} fusion(s32[512]{0:T(512)S(1)} %bitcast.98, bf16[512,2048]{1,0:T(8,128)(2,1)} %reshape.280, bf16[]{:T(256)} %constant.21.clone.1), kind=kCustom, calls=%fused_computation.37 | custom fusion | bytes 3146240 | tf_op jit(solution)/shard_map/scatter | solution.py:55
  74.8 33.7 %all-to-all-done.1 = bf16[16,48,2048]{2,1,0:T(8,128)(2,1)} async-done(((bf16[16,48,2048]{2,1,0:T(8,128)(2,1)}), bf16[16,48,2048]{2,1,0:T(8,128)(2,1)}, u32[]{:S(2)}, u32[]{:S(2)}) %all-to-all-start.1) | async-done | bytes 3145760 | tf_op jit(solution)/shard_map/all_to_all | solution.py:187
  108.5 16.2 %all-to-all-start = ((bf16[16,48,2048]{2,1,0:T(8,128)(2,1)}), bf16[16,48,2048]{2,1,0:T(8,128)(2,1)}, u32[]{:S(2)}, u32[]{:S(2)}) async-start(bf16[16,48,2048]{2,1,0:T(8,128)(2,1)} %bitcast.88), calls=%async_computation | async-start | bytes 6291456 | tf_op jit(solution)/shard_map/all_to_all | solution.py:194
  124.8 5.0 %fusion.7 = f32[768,512]{0,1:T(8,128)} fusion(bf16[768,2048]{1,0:T(8,128)(2,1)} %bitcast.11, bf16[1,2048,512]{2,1,0:T(8,128)(2,1)S(1)} %copy-done), kind=kOutput, calls=%fused_computation.19 | convolution fusion | flops 1610612736 | bytes 6815744 | tf_op jit(solution)/shard_map/esd,edh->esh/dot_general | solution.py:208
  129.8 4.9 %fusion.10 = f32[768,512]{0,1:T(8,128)} fusion(bf16[768,2048]{1,0:T(8,128)(2,1)} %bitcast.11, bf16[1,2048,512]{2,1,0:T(8,128)(2,1)S(1)} %copy-done.7), kind=kOutput, calls=%fused_computation.22 | convolution fusion | flops 1610612736 | bytes 6815744 | tf_op jit(solution)/shard_map/esd,edh->esh/dot_general | solution.py:209
  134.7 50.8 %all-to-all-done = bf16[16,48,2048]{2,1,0:T(8,128)(2,1)} async-done(((bf16[16,48,2048]{2,1,0:T(8,128)(2,1)}), bf16[16,48,2048]{2,1,0:T(8,128)(2,1)}, u32[]{:S(2)}, u32[]{:S(2)}) %all-to-all-start) | async-done | bytes 3145760 | tf_op jit(solution)/shard_map/all_to_all | solution.py:194
  185.5 6.5 %multiply_reduce_fusion = (f32[768]{0:T(1024)S(1)}, f32[768,512]{0,1:T(8,128)}) fusion(f32[768,512]{0,1:T(8,128)} %fusion.10, f32[768,512]{0,1:T(8,128)} %fusion.7, bf16[768,2048]{1,0:T(8,128)(2,1)} %bitcast.8, bf16[1,512,2048]{2,1,0:T(8,128)(2,1)} %param.19), kind=kOutput, calls=%fused_computation.31 | convolution fusion | flops 1613364480 | bytes 9964544 | tf_op jit(solution)/shard_map/esd,ehd->esh/dot_general | solution.py:210
  195.1 14.1 %all-to-all-start.3 = ((f32[16,1,48]{2,1,0:T(1,128)}), f32[16,1,48]{2,1,0:T(1,128)S(1)}, u32[]{:S(2)}, u32[]{:S(2)}) async-start(f32[16,1,48]{2,1,0:T(1,128)} %psum.21), calls=%async_computation.4 | async-start | bytes 16384 | tf_op jit(solution)/shard_map/all_to_all | solution.py:223
  209.3 4.8 %fusion.5 = f32[768,2048]{1,0:T(8,128)S(1)} fusion(bf16[1,2048,512]{2,1,0:T(8,128)(2,1)S(1)} %copy-done, f32[768,512]{0,1:T(8,128)} %fusion.7, f32[768,512]{0,1:T(8,128)} %get-tuple-element.25, f32[768,512]{0,1:T(8,128)} %fusion.10), kind=kOutput, calls=%fused_computation.17 | convolution fusion | flops 1614544896 | bytes 13107200 | tf_op jit(solution)/shard_map/esh,edh->esd/dot_general | solution.py:216
  217.7 7.0 %all-to-all-start.2 = ((bf16[16,48,2048]{2,1,0:T(8,128)(2,1)}), bf16[16,48,2048]{2,1,0:T(8,128)(2,1)S(1)}, u32[]{:S(2)}, u32[]{:S(2)}) async-start(bf16[16,48,2048]{2,1,0:T(8,128)(2,1)} %bitcast.89), calls=%async_computation.2 | async-start | bytes 6291456 | tf_op jit(solution)/shard_map/all_to_all | solution.py:220
  235.9 52.8 %all-to-all-done.2 = bf16[16,48,2048]{2,1,0:T(8,128)(2,1)S(1)} async-done(((bf16[16,48,2048]{2,1,0:T(8,128)(2,1)}), bf16[16,48,2048]{2,1,0:T(8,128)(2,1)S(1)}, u32[]{:S(2)}, u32[]{:S(2)}) %all-to-all-start.2) | async-done | bytes 3145760 | tf_op jit(solution)/shard_map/all_to_all | solution.py:220
  290.7 3.8 %scatter_custom_fusion.2 = bf16[768]{0:T(1024)(128)(2,1)S(1)} fusion(s32[512]{0:T(512)S(1)} %bitcast.100, bf16[512]{0:T(512)(128)(2,1)S(1)} %reshape.296, bf16[]{:T(256)} %constant.21.clone.1), kind=kCustom, calls=%fused_computation.82 | custom fusion | bytes 1538 | tf_op jit(solution)/shard_map/scatter | solution.py:57
  295.2 16.0 %all-to-all-start.4 = ((bf16[16,1,48]{2,1,0:T(2,128)(2,1)}), bf16[16,1,48]{2,1,0:T(2,128)(2,1)S(1)}, u32[]{:S(2)}, u32[]{:S(2)}) async-start(bf16[16,1,48]{2,1,0:T(2,128)(2,1)} %all_to_all.28), calls=%async_computation.5 | async-start | bytes 16384 | tf_op jit(solution)/shard_map/all_to_all | solution.py:201
  311.2 7.2 %all-to-all-done.4 = bf16[16,1,48]{2,1,0:T(2,128)(2,1)S(1)} async-done(((bf16[16,1,48]{2,1,0:T(2,128)(2,1)}), bf16[16,1,48]{2,1,0:T(2,128)(2,1)S(1)}, u32[]{:S(2)}, u32[]{:S(2)}) %all-to-all-start.4) | async-done | bytes 1568 | tf_op jit(solution)/shard_map/all_to_all | solution.py:201
  318.5 7.2 %fusion.2 = bf16[1,512,2048]{2,1,0:T(8,128)(2,1)} fusion(bf16[768,2048]{1,0:T(8,128)(2,1)} %bitcast.8, f32[768]{0:T(1024)S(1)} %reshape.259, f32[768,512]{0,1:T(8,128)} %fusion.10, f32[768,512]{0,1:T(8,128)} %fusion.7), kind=kOutput, calls=%fused_computation.14 | convolution fusion | flops 1614413824 | bytes 8391680 | tf_op jit(solution)/shard_map/esh,esd->ehd/dot_general | solution.py:86
  325.7 5.3 %fusion.1 = bf16[1,2048,512]{2,1,0:T(8,128)(2,1)} fusion(bf16[768,2048]{1,0:T(8,128)(2,1)} %bitcast.11, f32[768]{0:T(1024)S(1)} %reshape.259, f32[768,512]{0,1:T(8,128)S(1)} %copy-done.12, f32[768,512]{0,1:T(8,128)S(1)} %copy-done.10), kind=kOutput, calls=%fused_computation.13 | convolution fusion | flops 1614413824 | bytes 8391680 | tf_op jit(solution)/shard_map/esd,esh->edh/dot_general | solution.py:83
  331.0 5.2 %fusion = bf16[1,2048,512]{2,1,0:T(8,128)(2,1)} fusion(bf16[768,2048]{1,0:T(8,128)(2,1)} %bitcast.11, f32[768]{0:T(1024)S(1)} %reshape.259, f32[768,512]{0,1:T(8,128)S(1)} %copy-done.10, f32[768,512]{0,1:T(8,128)S(1)} %copy-done.12, f32[768,512]{0,1:T(8,128)S(1)} %copy-done.13), kind=kOutput, calls=%fused_computation.12 | convolution fusion | flops 1615986688 | bytes 9964544 | tf_op jit(solution)/shard_map/esd,esh->edh/dot_general | solution.py:80
  (99 shorter events, 58.2 us)
Async XLA Ops:
  7.2 117.6 %copy-start = (bf16[1,2048,512]{2,1,0:T(8,128)(2,1)S(1)}, bf16[1,2048,512]{2,1,0:T(8,128)(2,1)}, u32[]{:S(2)}) copy-start(bf16[1,2048,512]{2,1,0:T(8,128)(2,1)} %param.17) | copy-start | bytes 6291460
  7.2 14.1 %all-gather.5.cloned.1.call-start = ((), (), s32[]{:S(2)}) async-start(), calls=%async_computation.6 | async-start | bytes 1572864 | tf_op jit(solution)/shard_map/all_gather | solution.py:161
  40.2 7.7 %copy-start.6 = (bf16[1,1024]{1,0:T(2,128)(2,1)S(1)}, bf16[1,1024]{1,0:T(2,128)(2,1)}, u32[]{:S(2)}) copy-start(bf16[1,1024]{1,0:T(2,128)(2,1)} %param.16) | copy-start | bytes 6148
  40.2 68.3 %all-to-all-start.1 = ((bf16[16,48,2048]{2,1,0:T(8,128)(2,1)}), bf16[16,48,2048]{2,1,0:T(8,128)(2,1)}, u32[]{:S(2)}, u32[]{:S(2)}) async-start(bf16[16,48,2048]{2,1,0:T(8,128)(2,1)} %bitcast.87), calls=%async_computation.1 | async-start | bytes 6291456 | tf_op jit(solution)/shard_map/all_to_all | solution.py:187
  47.2 12.7 %all-gather.7.cloned.1.call-start = ((), (), s32[]{:S(2)}) async-start(), calls=%async_computation.7 | async-start | bytes 1572864 | tf_op jit(solution)/shard_map/all_gather | solution.py:162
  108.5 76.9 %all-to-all-start = ((bf16[16,48,2048]{2,1,0:T(8,128)(2,1)}), bf16[16,48,2048]{2,1,0:T(8,128)(2,1)}, u32[]{:S(2)}, u32[]{:S(2)}) async-start(bf16[16,48,2048]{2,1,0:T(8,128)(2,1)} %bitcast.88), calls=%async_computation | async-start | bytes 6291456 | tf_op jit(solution)/shard_map/all_to_all | solution.py:194
  124.8 5.0 %copy-start.7 = (bf16[1,2048,512]{2,1,0:T(8,128)(2,1)S(1)}, bf16[1,2048,512]{2,1,0:T(8,128)(2,1)}, u32[]{:S(2)}) copy-start(bf16[1,2048,512]{2,1,0:T(8,128)(2,1)} %param.18) | copy-start | bytes 6291460
  195.1 22.6 %all-to-all-start.3 = ((f32[16,1,48]{2,1,0:T(1,128)}), f32[16,1,48]{2,1,0:T(1,128)S(1)}, u32[]{:S(2)}, u32[]{:S(2)}) async-start(f32[16,1,48]{2,1,0:T(1,128)} %psum.21), calls=%async_computation.4 | async-start | bytes 16384 | tf_op jit(solution)/shard_map/all_to_all | solution.py:223
  209.2 4.8 %copy-start.8 = (bf16[1,2048,512]{2,1,0:T(8,128)(2,1)S(1)}, bf16[1,2048,512]{2,1,0:T(8,128)(2,1)}, u32[]{:S(2)}) copy-start(bf16[1,2048,512]{2,1,0:T(8,128)(2,1)} %param.18) | copy-start | bytes 6291460
  209.3 4.8 %copy-start.9 = (f32[768,512]{0,1:T(8,128)S(1)}, f32[768,512]{0,1:T(8,128)}, u32[]{:S(2)}) copy-start(f32[768,512]{0,1:T(8,128)} %fusion.7) | copy-start | bytes 4718596
  209.3 4.8 %copy-start.11 = (f32[768,512]{0,1:T(8,128)S(1)}, f32[768,512]{0,1:T(8,128)}, u32[]{:S(2)}) copy-start(f32[768,512]{0,1:T(8,128)} %get-tuple-element.25) | copy-start | bytes 4718596
  217.7 7.1 %copy-start.4 = (f32[1024,16]{0,1:T(8,128)S(1)}, f32[1024,16]{0,1:T(8,128)}, u32[]{:S(2)}) copy-start(f32[1024,16]{0,1:T(8,128)} %param.13) | copy-start | bytes 196612
  217.7 71.0 %all-to-all-start.2 = ((bf16[16,48,2048]{2,1,0:T(8,128)(2,1)}), bf16[16,48,2048]{2,1,0:T(8,128)(2,1)S(1)}, u32[]{:S(2)}, u32[]{:S(2)}) async-start(bf16[16,48,2048]{2,1,0:T(8,128)(2,1)} %bitcast.89), calls=%async_computation.2 | async-start | bytes 6291456 | tf_op jit(solution)/shard_map/all_to_all | solution.py:220
  224.7 4.6 %copy-start.5 = (s32[256,2]{0,1:T(2,128)S(1)}, s32[256,2]{0,1:T(2,128)}, u32[]{:S(2)}) copy-start(s32[256,2]{0,1:T(2,128)} %param.12) | copy-start | bytes 6148
  224.8 111.4 %all-gather.9.cloned.1.call-start = ((), (), s32[]{:S(2)}) async-start(), calls=%async_computation.9 | async-start | bytes 1114112 | tf_op jit(solution)/shard_map/all_gather | solution.py:121
  235.8 103.0 %reduce-scatter.2.cloned.1.call-start = ((), (), s32[]{:S(2)}) async-start(), calls=%async_computation.8 | async-start | bytes 4718592 | tf_op jit(solution)/shard_map/reduce_scatter | solution.py:226
  288.7 1.7 copy-start.2
  295.2 23.3 %all-to-all-start.4 = ((bf16[16,1,48]{2,1,0:T(2,128)(2,1)}), bf16[16,1,48]{2,1,0:T(2,128)(2,1)S(1)}, u32[]{:S(2)}, u32[]{:S(2)}) async-start(bf16[16,1,48]{2,1,0:T(2,128)(2,1)} %all_to_all.28), calls=%async_computation.5 | async-start | bytes 16384 | tf_op jit(solution)/shard_map/all_to_all | solution.py:201
  318.5 7.2 %copy-start.10 = (f32[768,512]{0,1:T(8,128)S(1)}, f32[768,512]{0,1:T(8,128)}, u32[]{:S(2)}) copy-start(f32[768,512]{0,1:T(8,128)} %fusion.7) | copy-start | bytes 4718596
  318.5 7.2 %copy-start.12 = (f32[768,512]{0,1:T(8,128)S(1)}, f32[768,512]{0,1:T(8,128)}, u32[]{:S(2)}) copy-start(f32[768,512]{0,1:T(8,128)} %get-tuple-element.25) | copy-start | bytes 4718596
  325.7 5.3 %copy-start.13 = (f32[768,512]{0,1:T(8,128)S(1)}, f32[768,512]{0,1:T(8,128)}, u32[]{:S(2)}) copy-start(f32[768,512]{0,1:T(8,128)} %fusion.10) | copy-start | bytes 4718596
  345.8 1.6 copy-start.3
  347.5 6.5 %copy-start.1 = (bf16[1,2048,512]{2,1,0:T(8,128)(2,1)S(1)}, bf16[1,2048,512]{2,1,0:T(8,128)(2,1)}, u32[]{:S(2)}) copy-start(bf16[1,2048,512]{2,1,0:T(8,128)(2,1)} %param.17) | copy-start | bytes 6291460
Sparse Core Ops, SparseCore 0:
  9.5 11.7 all-gather.4
  49.6 10.2 all-gather.6
  235.9 76.7 all-gather.8
  314.8 9.7 reduce-scatter.1
